TPU v7x, 256 devices: a whole 4x4x8 slice. The times are simulated.
256 devices in a mesh: blk: 32 (over z_hi, y, core), head: 8 (over z_lo, x).
Axes of the slice: x: 4, y: 4, z: 8 (z_hi: 4, z_lo: 2; z = z_hi * 2 + z_lo), core: 2. Of those that a mesh axis runs over, the one named last changes fastest.
Arguments:
- query: bfloat16 [32768, 3072], P(('blk', 'head')), may hold values from -6 to 6
- keys: bfloat16 [32768, 3072], P(('blk', 'head')), may hold values from -6 to 6
- values: bfloat16 [32768, 3072], P(('blk', 'head')), may hold values from -6 to 6
- cotangent: bfloat16 [32768, 3072], P(('blk', 'head')), may hold values from -6 to 6
- kv_tiles: int32 [24, 256, 9], P('head'), may hold values from 0 to 255, as said below
Outputs:
- attended: bfloat16 [32768, 3072], P(('blk', 'head'))
- d_query: bfloat16 [32768, 3072], P(('blk', 'head'))
- d_keys: bfloat16 [32768, 3072], P(('blk', 'head'))
- d_values: bfloat16 [32768, 3072], P(('blk', 'head'))
Inputs may be any that keep to these rules, and one draw needn't show every extreme that they name: `kv_tiles`: the 9 entries of a row are distinct; the first 2 entries are the same in every row of one head (that head's global tiles); every other entry lies within 8 tiles of the row's query tile and is not a global tile of that head.
All inputs are finite; a program needn't handle non-finite values.
Results may differ from a plain program's by a relative error of at most 0.017.
Values may be sent and summed in bfloat16 or wider, within the bound.
A program may use at most 192 MiB of HBM per device.

v0:
```python
import jax
import jax.numpy as jnp
from jax import lax
from jax.sharding import PartitionSpec as P

HD = 128
TILE = 128
GLOBALS = 2
HALF = 8


def passed_along(block, axis, distance):
    devices = range(lax.axis_size(axis))
    route = [(i - distance, i) for i in devices if i - distance in devices]
    return lax.ppermute(block, axis, route)


def split_heads(field, count):
    heads = field.shape[1] // HD
    return field.reshape(count, TILE, heads, HD).transpose(2, 0, 1, 3)


def merge_heads(field):
    heads = field.shape[0]
    count = field.shape[1]
    return field.transpose(1, 2, 0, 3).reshape(count * TILE, heads * HD)


def recompute_probs(queries, chosen_keys, log_total):
    scale = HD ** (-0.5)
    scores = (
        jnp.einsum("tqd,tskd->tqsk", queries, chosen_keys, preferred_element_type=jnp.float32)
        * scale
    )
    return jnp.exp(scores - log_total)


def attend_forward(item):
    queries, pool_keys, pool_values, pool_index = item
    scale = HD ** (-0.5)
    chosen_keys = jnp.take(pool_keys, pool_index, axis=0)
    chosen_values = jnp.take(pool_values, pool_index, axis=0)
    scores = (
        jnp.einsum("tqd,tskd->tqsk", queries, chosen_keys, preferred_element_type=jnp.float32)
        * scale
    )
    peak = jnp.max(scores, axis=(2, 3), keepdims=True)
    log_total = peak + jnp.log(jnp.sum(jnp.exp(scores - peak), axis=(2, 3), keepdims=True))
    weights = jnp.exp(scores - log_total).astype(jnp.bfloat16)
    attended = jnp.einsum(
        "tqsk,tskd->tqd", weights, chosen_values, preferred_element_type=jnp.float32
    )
    return (attended.astype(jnp.bfloat16), log_total)


def attend_backward(item):
    queries, pool_keys, pool_values, grad_out, attended, log_total, pool_index = item
    scale = HD ** (-0.5)
    chosen_keys = jnp.take(pool_keys, pool_index, axis=0)
    chosen_values = jnp.take(pool_values, pool_index, axis=0)
    probs = recompute_probs(queries, chosen_keys, log_total)
    weights = probs.astype(jnp.bfloat16)
    delta = jnp.sum(grad_out.astype(jnp.float32) * attended.astype(jnp.float32), axis=-1)
    grad_probs = jnp.einsum(
        "tqd,tskd->tqsk", grad_out, chosen_values, preferred_element_type=jnp.float32
    )
    grad_scores = (probs * (grad_probs - delta[:, :, None, None])).astype(jnp.bfloat16)
    grad_query = (
        jnp.einsum("tqsk,tskd->tqd", grad_scores, chosen_keys, preferred_element_type=jnp.float32)
        * scale
    )
    key_slots = (
        jnp.einsum("tqsk,tqd->tskd", grad_scores, queries, preferred_element_type=jnp.float32)
        * scale
    )
    value_slots = jnp.einsum(
        "tqsk,tqd->tskd", weights, grad_out, preferred_element_type=jnp.float32
    )
    slot_count = pool_index.shape[0] * pool_index.shape[1]
    places = (
        pool_index.reshape(-1)[:, None] == jnp.arange(pool_keys.shape[0], dtype=jnp.int32)[None, :]
    ).astype(jnp.float32)
    key_pool = jnp.einsum(
        "sp,skd->pkd",
        places,
        key_slots.reshape(slot_count, TILE, HD),
        precision=lax.Precision.HIGHEST,
    )
    value_pool = jnp.einsum(
        "sp,skd->pkd",
        places,
        value_slots.reshape(slot_count, TILE, HD),
        precision=lax.Precision.HIGHEST,
    )
    return (grad_query.astype(jnp.bfloat16), key_pool, value_pool)


def per_device(query, keys, values, cotangent, kv_tiles):
    head_count = lax.axis_size("head")
    cycle_pos = lax.axis_index("blk")
    per_frame = query.shape[0] * head_count // TILE
    reach = -(-HALF // per_frame)
    span = (2 * reach + 1) * per_frame
    global_tiles = kv_tiles[:, 0, :GLOBALS]
    own_tiles = lax.dynamic_slice_in_dim(kv_tiles, cycle_pos * per_frame, per_frame, 1)
    moved = (
        lax.all_to_all(query, "head", split_axis=1, concat_axis=0, tiled=True),
        lax.all_to_all(keys, "head", split_axis=1, concat_axis=0, tiled=True),
        lax.all_to_all(values, "head", split_axis=1, concat_axis=0, tiled=True),
        lax.all_to_all(cotangent, "head", split_axis=1, concat_axis=0, tiled=True),
    )
    frame_keys = moved[1]
    frame_values = moved[2]
    offset = 1
    earlier = passed_along((frame_keys, frame_values), "blk", offset)
    later = passed_along((frame_keys, frame_values), "blk", -offset)
    earlier_keys = [earlier[0]]
    earlier_values = [earlier[1]]
    later_keys = [later[0]]
    later_values = [later[1]]
    near_keys = jnp.stack(earlier_keys[::-1] + later_keys, axis=0)
    near_values = jnp.stack(earlier_values[::-1] + later_values, axis=0)
    width = frame_keys.shape[1]
    all_keys = jnp.concatenate(
        [near_keys[:reach], frame_keys[None], near_keys[reach:]], axis=0
    ).reshape(span * TILE, width)
    all_values = jnp.concatenate(
        [near_values[:reach], frame_values[None], near_values[reach:]], axis=0
    ).reshape(span * TILE, width)
    own_keys = split_heads(frame_keys, per_frame)
    own_values = split_heads(frame_values, per_frame)
    tile_ids = cycle_pos * per_frame + jnp.arange(per_frame, dtype=jnp.int32)
    owner = global_tiles[:, :, None] == tile_ids[None, None, :]
    owner_mask = owner.astype(jnp.bfloat16)
    global_keys = jnp.einsum(
        "hjt,htkd->hjkd", owner_mask, own_keys, preferred_element_type=jnp.float32
    )
    global_values = jnp.einsum(
        "hjt,htkd->hjkd", owner_mask, own_values, preferred_element_type=jnp.float32
    )
    global_keys, global_values = (
        lax.psum(global_keys.astype(jnp.bfloat16), "blk").astype(jnp.float32),
        lax.psum(global_values.astype(jnp.bfloat16), "blk").astype(jnp.float32),
    )
    pool_keys = jnp.concatenate(
        [split_heads(all_keys, span), global_keys.astype(jnp.bfloat16)], axis=1
    )
    pool_values = jnp.concatenate(
        [split_heads(all_values, span), global_values.astype(jnp.bfloat16)], axis=1
    )
    relative = own_tiles - (cycle_pos - reach) * per_frame
    inside = (relative >= 0) & (relative < span)
    matches = own_tiles[:, :, :, None] == global_tiles[:, None, None, :]
    slot_numbers = jnp.arange(global_tiles.shape[1], dtype=jnp.int32)
    global_slot = jnp.sum(jnp.where(matches, slot_numbers[None, None, None, :], 0), axis=-1)
    pool_index = jnp.where(inside, relative, span + global_slot)
    queries = split_heads(moved[0], per_frame)
    grad_out = split_heads(moved[3], per_frame)
    attended, log_total = lax.map(attend_forward, (queries, pool_keys, pool_values, pool_index))
    grad_query, key_pool, value_pool = lax.map(
        attend_backward,
        (queries, pool_keys, pool_values, grad_out, attended, log_total, pool_index),
    )
    centre = reach * per_frame
    key_grad = key_pool[:, centre : centre + per_frame]
    value_grad = value_pool[:, centre : centre + per_frame]
    offset = 1
    lower = (reach - offset) * per_frame
    returned = (
        passed_along(
            key_pool[:, lower : lower + per_frame].astype(jnp.bfloat16), "blk", -offset
        ).astype(jnp.float32),
        passed_along(
            value_pool[:, lower : lower + per_frame].astype(jnp.bfloat16), "blk", -offset
        ).astype(jnp.float32),
    )
    key_grad = key_grad + returned[0]
    value_grad = value_grad + returned[1]
    upper = (reach + offset) * per_frame
    returned = (
        passed_along(
            key_pool[:, upper : upper + per_frame].astype(jnp.bfloat16), "blk", offset
        ).astype(jnp.float32),
        passed_along(
            value_pool[:, upper : upper + per_frame].astype(jnp.bfloat16), "blk", offset
        ).astype(jnp.float32),
    )
    key_grad = key_grad + returned[0]
    value_grad = value_grad + returned[1]
    summed = (
        lax.psum(key_pool[:, span:].astype(jnp.bfloat16), "blk").astype(jnp.float32),
        lax.psum(value_pool[:, span:].astype(jnp.bfloat16), "blk").astype(jnp.float32),
    )
    owner_float = owner.astype(jnp.float32)
    key_grad = key_grad + jnp.einsum(
        "hjt,hjkd->htkd", owner_float, summed[0], precision=lax.Precision.HIGHEST
    )
    value_grad = value_grad + jnp.einsum(
        "hjt,hjkd->htkd", owner_float, summed[1], precision=lax.Precision.HIGHEST
    )
    query_rows = merge_heads(grad_query)
    key_rows = merge_heads(key_grad.astype(jnp.bfloat16))
    value_rows = merge_heads(value_grad.astype(jnp.bfloat16))
    results = (
        lax.all_to_all(merge_heads(attended), "head", split_axis=0, concat_axis=1, tiled=True),
        lax.all_to_all(query_rows, "head", split_axis=0, concat_axis=1, tiled=True),
        lax.all_to_all(key_rows, "head", split_axis=0, concat_axis=1, tiled=True),
        lax.all_to_all(value_rows, "head", split_axis=0, concat_axis=1, tiled=True),
    )
    return (results[0], results[1], results[2], results[3])


def solution(mesh):
    placed = (
        P(("blk", "head"), None),
        P(("blk", "head"), None),
        P(("blk", "head"), None),
        P(("blk", "head"), None),
        P("head", None, None),
    )
    return jax.shard_map(
        per_device,
        mesh=mesh,
        in_specs=placed,
        out_specs=(
            P(("blk", "head"), None),
            P(("blk", "head"), None),
            P(("blk", "head"), None),
            P(("blk", "head"), None),
        ),
        check_vma=False,
    )
```

profile of v0, /device:TPU:160, one launch (start us, length us, event | category | flops | bytes accessed | tf_op | source)
XLA Modules:
  0.0 897.8 jit_solution(17046188124416074661)
XLA Ops:
  7.2 2.4 copy.91
  9.5 5.9 all-to-all-start.1
  16.6 10.3 %all-to-all-done.1 = bf16[128,8,384]{0,2,1:T(8,128)(2,1)S(1)} async-done(((bf16[128,8,384]{0,2,1:T(8,128)(2,1)}), bf16[128,8,384]{0,2,1:T(8,128)(2,1)S(1)}, u32[]{:S(2)}, u32[]{:S(2)}) %all-to-all-start.1) | async-done | bytes 786464 | tf_op jit(solution)/shard_map/all_to_all | solution.py:108
  26.9 4.2 all-to-all-start.2
  32.2 10.5 %all-to-all-done.2 = bf16[128,8,384]{0,2,1:T(8,128)(2,1)S(1)} async-done(((bf16[128,8,384]{0,2,1:T(8,128)(2,1)}), bf16[128,8,384]{0,2,1:T(8,128)(2,1)S(1)}, u32[]{:S(2)}, u32[]{:S(2)}) %all-to-all-start.2) | async-done | bytes 786464 | tf_op jit(solution)/shard_map/all_to_all | solution.py:109
  42.7 4.2 all-to-all-start
  47.4 4.0 collective-permute-start.3
  61.8 7.8 collective-permute-start.1
  72.8 6.1 all-to-all-start.4
  80.1 262.5 %all-reduce.7.cloned.1.call-done = (bf16[3,2,128,128]{3,1,2,0:T(2,128)(2,1)}, bf16[3,2,128,128]{3,1,2,0:T(2,128)(2,1)}) async-done(((bf16[3,2,128,128]{3,1,2,0:T(2,128)(2,1)}, bf16[3,2,128,128]{3,1,2,0:T(2,128)(2,1)}), (bf16[3,2,128,128]{3,1,2,0:T(2,128)(2,1)}, bf16[3,2,128,128]{3,1,2,0:T(2,128)(2,1)})) %all-reduce.7.cloned.1.call-update) | async-done | bytes 393232 | tf_op jit(solution)/shard_map/psum | solution.py:142
  345.5 3.1 pad_maximum_fusion.3
  348.6 5.9 reshape_reshape.7
  354.5 3.1 pad_maximum_fusion.1
  359.8 3.3 pad_maximum_fusion.2
  363.1 5.9 reshape_reshape.6
  373.4 32.2 %while.26 = (s32[]{:T(128)}, bf16[3,8,128,128]{3,2,1,0:T(8,128)(2,1)}, f32[3,8,128,1,1]{2,1,4,3,0:T(8,128)S(1)}, bf16[3,8,128,128]{3,2,1,0:T(8,128)(2,1)}, bf16[...) while((s32[]{:T(128)}, ...), condition=%wide.region_6.8_spmd, body=%wide.region_3.7_spmd.sunk | while | flops 615907776 | bytes 41720132 | solution.py:159
  375.0 2.4 gather_fusion
  385.7 2.4 gather_fusion
  396.5 2.4 gather_fusion
  407.9 5.7 all-to-all-start.3
  413.6 115.5 %while.27 = (s32[]{:T(128)}, bf16[3,8,128,128]{2,3,0,1:T(8,128)(2,1)}, f32[3,26,128,128]{3,1,2,0:T(8,128)}, f32[3,26,128,128]{3,1,2,0:T(8,128)}, bf16[3,8,128,12...) while((s32[]{:T(128)}, ...), condition=%wide.region_9.11_spmd, body=%wide.region_7.10_spmd.sunk | while | flops 2260996352 | bytes 105939144 | solution.py:160
  428.3 2.4 gather_fusion.2
  430.7 2.4 gather_fusion.3
  438.7 3.4 fusion.140
  443.1 8.2 bitcast_dynamic-update-slice_fusion.8
  453.2 6.0 bitcast_dynamic-update-slice_fusion.7
  463.2 2.4 gather_fusion.2
  465.7 2.4 gather_fusion.3
  473.7 3.4 fusion.140
  478.0 8.2 bitcast_dynamic-update-slice_fusion.8
  488.1 6.0 bitcast_dynamic-update-slice_fusion.7
  498.1 2.4 gather_fusion.2
  500.5 2.4 gather_fusion.3
  508.6 3.4 fusion.140
  512.9 8.2 bitcast_dynamic-update-slice_fusion.8
  523.0 6.0 bitcast_dynamic-update-slice_fusion.7
  529.0 3.5 convert.12
  532.6 5.7 all-to-all-start.5
  539.7 3.4 collective-permute-start.6
  545.8 3.6 convert.11
  550.2 279.6 %all-reduce.5.cloned.1.call-done = (bf16[3,2,128,128]{3,1,2,0:T(2,128)(2,1)}, bf16[3,2,128,128]{3,1,2,0:T(2,128)(2,1)}) async-done(((bf16[3,2,128,128]{3,1,2,0:T(2,128)(2,1)}, bf16[3,2,128,128]{3,1,2,0:T(2,128)(2,1)}), (bf16[3,2,128,128]{3,1,2,0:T(2,128)(2,1)}, bf16[3,2,128,128]{3,1,2,0:T(2,128)(2,1)})) %all-reduce.5.cloned.1.call-update) | async-done | bytes 393232 | tf_op jit(solution)/shard_map/psum | solution.py:191
  829.8 3.5 fusion.74
  833.3 2.4 copy.115
  835.7 5.8 all-to-all-start.7
  841.8 3.9 collective-permute-start.4
  847.7 13.1 %collective-permute-done.4 = bf16[3,8,128,128]{3,1,2,0:T(8,128)(2,1)S(1)} collective-permute-done((bf16[3,8,128,128]{3,1,2,0:T(8,128)(2,1)S(1)}, bf16[3,8,128,128]{3,1,2,0:T(8,128)(2,1)S(1)}, u32[]{:S(2)}, u32[]{:S(2)}) %collective-permute-start.4) | collective-permute-done | bytes 786464 | tf_op jit(solution)/shard_map/ppermute | solution.py:15
  860.8 11.0 %collective-permute-done.5 = bf16[3,8,128,128]{3,1,2,0:T(8,128)(2,1)S(1)} collective-permute-done((bf16[3,8,128,128]{3,1,2,0:T(8,128)(2,1)S(1)}, bf16[3,8,128,128]{3,1,2,0:T(8,128)(2,1)S(1)}, u32[]{:S(2)}, u32[]{:S(2)}) %collective-permute-start.5) | collective-permute-done | bytes 786464 | tf_op jit(solution)/shard_map/ppermute | solution.py:15
  875.2 5.7 all-to-all-start.6
  (181 shorter events, 111.8 us)
Async XLA Ops:
  7.2 8.3 copy-start.5
  9.5 21.5 %copy-start.6 = (bf16[128,3072]{1,0:T(8,128)(2,1)S(1)}, bf16[128,3072]{1,0:T(8,128)(2,1)}, u32[]{:S(2)}) copy-start(bf16[128,3072]{1,0:T(8,128)(2,1)} %param.11) | copy-start | bytes 2359300
  9.5 17.3 %all-to-all-start.1 = ((bf16[128,8,384]{0,2,1:T(8,128)(2,1)}), bf16[128,8,384]{0,2,1:T(8,128)(2,1)S(1)}, u32[]{:S(2)}, u32[]{:S(2)}) async-start(bf16[128,8,384]{0,2,1:T(8,128)(2,1)} %bitcast.39), calls=%async_computation.1 | async-start | bytes 1572864 | tf_op jit(solution)/shard_map/all_to_all | solution.py:108
  16.6 30.3 %copy-start.11 = (s32[3,256,9]{1,0,2:T(4,128)S(1)}, s32[3,256,9]{1,0,2:T(4,128)}, u32[]{:S(2)}) copy-start(s32[3,256,9]{1,0,2:T(4,128)} %param.15) | copy-start | bytes 82948
  26.9 15.8 %all-to-all-start.2 = ((bf16[128,8,384]{0,2,1:T(8,128)(2,1)}), bf16[128,8,384]{0,2,1:T(8,128)(2,1)S(1)}, u32[]{:S(2)}, u32[]{:S(2)}) async-start(bf16[128,8,384]{0,2,1:T(8,128)(2,1)} %bitcast.50), calls=%async_computation.2 | async-start | bytes 1572864 | tf_op jit(solution)/shard_map/all_to_all | solution.py:109
  42.7 30.2 %all-to-all-start = ((bf16[128,8,384]{0,2,1:T(8,128)(2,1)}), bf16[128,8,384]{0,2,1:T(8,128)(2,1)S(1)}, u32[]{:S(2)}, u32[]{:S(2)}) async-start(bf16[128,8,384]{0,2,1:T(8,128)(2,1)} %bitcast.35), calls=%async_computation | async-start | bytes 1572864 | tf_op jit(solution)/shard_map/all_to_all | solution.py:107
  46.9 295.8 %all-reduce.7.cloned.1.call-start = ((), (), s32[]{:S(2)}) async-start(), calls=%async_computation.9 | async-start | bytes 786432 | tf_op jit(solution)/shard_map/psum | solution.py:142
  47.0 13.6 %copy-start.9 = (s32[3,1,2]{2,0,1:T(4,128)}, s32[3,1,2]{2,0,1:T(4,128)S(1)}, u32[]{:S(2)}) copy-start(s32[3,1,2]{2,0,1:T(4,128)S(1)} %copy.129) | copy-start | bytes 76
  47.0 11.1 %copy-start.12 = (s32[8]{0:T(128)}, s32[8]{0:T(128)S(1)}, u32[]{:S(2)}) copy-start(s32[8]{0:T(128)S(1)} %iota_add_fusion) | copy-start | bytes 100
  47.4 298.2 %collective-permute-start.3 = (bf16[1024,384]{1,0:T(8,128)(2,1)S(1)}, bf16[1024,384]{1,0:T(8,128)(2,1)}, u32[]{:S(2)}, u32[]{:S(2)}) collective-permute-start(bf16[1024,384]{1,0:T(8,128)(2,1)S(1)} %bitcast.238), channel_id=1, source_target_pairs={{8,0},{16,8},{24,16},{32,24},{40,32},{48,40},{56,48},{64,56},{72,6... | collective-permute-start | bytes 2359304 | tf_op jit(solution)/shard_map/ppermute | solution.py:15
  51.3 294.2 %collective-permute-start.2 = (bf16[1024,384]{1,0:T(8,128)(2,1)S(1)}, bf16[1024,384]{1,0:T(8,128)(2,1)}, u32[]{:S(2)}, u32[]{:S(2)}) collective-permute-start(bf16[1024,384]{1,0:T(8,128)(2,1)S(1)} %bitcast.239), channel_id=1, source_target_pairs={{0,8},{8,16},{16,24},{24,32},{32,40},{40,48},{48,56},{56,64},{64,7... | collective-permute-start | bytes 2359304 | tf_op jit(solution)/shard_map/ppermute | solution.py:15
  58.1 13.6 %copy-start.7 = (bf16[128,3072]{1,0:T(8,128)(2,1)S(1)}, bf16[128,3072]{1,0:T(8,128)(2,1)}, u32[]{:S(2)}) copy-start(bf16[128,3072]{1,0:T(8,128)(2,1)} %param.14) | copy-start | bytes 2359300
  61.8 298.0 %collective-permute-start.1 = (bf16[1024,384]{1,0:T(8,128)(2,1)}, bf16[1024,384]{1,0:T(8,128)(2,1)}, u32[]{:S(2)}, u32[]{:S(2)}) collective-permute-start(bf16[1024,384]{1,0:T(8,128)(2,1)} %bitcast.41), channel_id=1, source_target_pairs={{8,0},{16,8},{24,16},{32,24},{40,32},{48,40},{56,48},{64,56},{72,6... | collective-permute-start | bytes 2359304 | tf_op jit(solution)/shard_map/ppermute | solution.py:15
  69.7 290.2 %collective-permute-start = (bf16[1024,384]{1,0:T(8,128)(2,1)}, bf16[1024,384]{1,0:T(8,128)(2,1)}, u32[]{:S(2)}, u32[]{:S(2)}) collective-permute-start(bf16[1024,384]{1,0:T(8,128)(2,1)} %bitcast.41), channel_id=1, source_target_pairs={{0,8},{8,16},{16,24},{24,32},{32,40},{40,48},{48,56},{56,64},{64,7... | collective-permute-start | bytes 2359304 | tf_op jit(solution)/shard_map/ppermute | solution.py:15
  72.8 335.0 %all-to-all-start.4 = ((bf16[128,8,384]{0,2,1:T(8,128)(2,1)}), bf16[128,8,384]{0,2,1:T(8,128)(2,1)}, u32[]{:S(2)}, u32[]{:S(2)}) async-start(bf16[128,8,384]{0,2,1:T(8,128)(2,1)} %bitcast.66), calls=%async_computation.4 | async-start | bytes 1572864 | tf_op jit(solution)/shard_map/all_to_all | solution.py:110
  380.3 1.7 copy-start.1
  391.0 1.7 copy-start.1
  401.7 1.7 copy-start.1
  407.9 124.7 %all-to-all-start.3 = ((bf16[8,128,384]{1,2,0:T(8,128)(2,1)}), bf16[8,128,384]{1,2,0:T(8,128)(2,1)}, u32[]{:S(2)}, u32[]{:S(2)}) async-start(bf16[8,128,384]{1,2,0:T(8,128)(2,1)} %bitcast.61), calls=%async_computation.3 | async-start | bytes 1572864 | tf_op jit(solution)/shard_map/all_to_all | solution.py:205
  430.7 2.4 copy-start
  433.1 2.0 copy-start.2
  437.3 1.4 copy-start.3
  443.1 8.2 copy-start.4
  465.6 2.4 copy-start
  468.1 2.1 copy-start.2
  472.3 1.4 copy-start.3
  478.0 8.2 copy-start.4
  500.5 2.4 copy-start
  502.9 2.1 copy-start.2
  507.1 1.4 copy-start.3
  512.9 8.2 copy-start.4
  532.6 303.1 %all-to-all-start.5 = ((bf16[8,128,384]{1,2,0:T(8,128)(2,1)}), bf16[8,128,384]{1,2,0:T(8,128)(2,1)}, u32[]{:S(2)}, u32[]{:S(2)}) async-start(bf16[8,128,384]{1,2,0:T(8,128)(2,1)} %bitcast.244), calls=%async_computation.5 | async-start | bytes 1572864 | tf_op jit(solution)/shard_map/all_to_all | solution.py:206
  538.3 291.5 %all-reduce.5.cloned.1.call-start = ((), (), s32[]{:S(2)}) async-start(), calls=%async_computation.8 | async-start | bytes 786432 | tf_op jit(solution)/shard_map/psum | solution.py:191
  539.7 290.1 %collective-permute-start.6 = (bf16[3,8,128,128]{3,1,2,0:T(8,128)(2,1)}, bf16[3,8,128,128]{3,1,2,0:T(8,128)(2,1)}, u32[]{:S(2)}, u32[]{:S(2)}) collective-permute-start(bf16[3,8,128,128]{3,1,2,0:T(8,128)(2,1)} %get-tuple-element.225), channel_id=1, source_target_pairs={{8,0},{16,8},{24,16},{32,24},{40,32},{48,40},{56,48},{64,56},{72,6... | collective-permute-start | bytes 2359304 | tf_op jit(solution)/shard_map/ppermute | solution.py:15
  543.1 286.7 %collective-permute-start.7 = (bf16[3,8,128,128]{3,1,2,0:T(8,128)(2,1)}, bf16[3,8,128,128]{3,1,2,0:T(8,128)(2,1)}, u32[]{:S(2)}, u32[]{:S(2)}) collective-permute-start(bf16[3,8,128,128]{3,1,2,0:T(8,128)(2,1)} %get-tuple-element.226), channel_id=1, source_target_pairs={{0,8},{8,16},{16,24},{24,32},{32,40},{40,48},{48,56},{56,64},{64,7... | collective-permute-start | bytes 2359304 | tf_op jit(solution)/shard_map/ppermute | solution.py:15
  545.8 284.0 %copy-start.10 = (s32[3,1,2]{2,0,1:T(4,128)S(1)}, s32[3,1,2]{2,0,1:T(4,128)}, u32[]{:S(2)}) copy-start(s32[3,1,2]{2,0,1:T(4,128)} %copy-done.9) | copy-start | bytes 76
  545.8 284.0 %copy-start.13 = (s32[8]{0:T(128)S(1)}, s32[8]{0:T(128)}, u32[]{:S(2)}) copy-start(s32[8]{0:T(128)} %copy-done.12) | copy-start | bytes 100
  835.7 36.1 %copy-start.8 = (bf16[3,2,128,128]{3,1,2,0:T(2,128)(2,1)S(1)}, bf16[3,2,128,128]{3,1,2,0:T(2,128)(2,1)}, u32[]{:S(2)}) copy-start(bf16[3,2,128,128]{3,1,2,0:T(2,128)(2,1)} %get-tuple-element.209) | copy-start | bytes 589828
  835.7 39.6 %all-to-all-start.7 = ((bf16[8,128,384]{1,2,0:T(8,128)(2,1)}), bf16[8,128,384]{1,2,0:T(8,128)(2,1)}, u32[]{:S(2)}, u32[]{:S(2)}) async-start(bf16[8,128,384]{1,2,0:T(8,128)(2,1)} %bitcast.242), calls=%async_computation.7 | async-start | bytes 1572864 | tf_op jit(solution)/shard_map/all_to_all | solution.py:208
  841.8 19.0 %collective-permute-start.4 = (bf16[3,8,128,128]{3,1,2,0:T(8,128)(2,1)S(1)}, bf16[3,8,128,128]{3,1,2,0:T(8,128)(2,1)S(1)}, u32[]{:S(2)}, u32[]{:S(2)}) collective-permute-start(bf16[3,8,128,128]{3,1,2,0:T(8,128)(2,1)S(1)} %get-tuple-element.227), channel_id=1, source_target_pairs={{8,0},{16,8},{24,16},{32,24},{40,32},{48,40},{56,48},{64,56},{72,6... | collective-permute-start | bytes 2359304 | tf_op jit(solution)/shard_map/ppermute | solution.py:15
  845.7 26.1 %collective-permute-start.5 = (bf16[3,8,128,128]{3,1,2,0:T(8,128)(2,1)S(1)}, bf16[3,8,128,128]{3,1,2,0:T(8,128)(2,1)S(1)}, u32[]{:S(2)}, u32[]{:S(2)}) collective-permute-start(bf16[3,8,128,128]{3,1,2,0:T(8,128)(2,1)S(1)} %get-tuple-element.228), channel_id=1, source_target_pairs={{0,8},{8,16},{16,24},{24,32},{32,40},{40,48},{48,56},{56,64},{64,7... | collective-permute-start | bytes 2359304 | tf_op jit(solution)/shard_map/ppermute | solution.py:15
  875.2 14.3 %all-to-all-start.6 = ((bf16[8,128,384]{1,2,0:T(8,128)(2,1)}), bf16[8,128,384]{1,2,0:T(8,128)(2,1)S(1)}, u32[]{:S(2)}, u32[]{:S(2)}) async-start(bf16[8,128,384]{1,2,0:T(8,128)(2,1)} %bitcast.75), calls=%async_computation.6 | async-start | bytes 1572864 | tf_op jit(solution)/shard_map/all_to_all | solution.py:207
Sparse Core Ops, SparseCore 0:
  60.5 282.0 all-reduce.6
  550.3 279.4 all-reduce.4
where the time goes:
time: 904 us; the launch traced here: 898 us
  waiting for transfers between devices  589 us (65%)
  matrix products  95.7 us (11%)
  local copies, waits for them, and re-layouts  92.7 us (10%)
  starting transfers between devices  70.2 us (8%)
  other arithmetic  24.9 us (3%)
  between operations  14.5 us (2%)
  loops' own time  11 us (1%)
    psum x1, waiting for transfers between devices, per_device(): lax.psum(key_pool[:, span:].astype(jnp.bfloat16), 'blk').astype(jnp.float32)  280 us
    psum x1, waiting for transfers between devices, per_device(): lax.psum(global_keys.astype(jnp.bfloat16), 'blk').astype(jnp.float32)  262 us
    ppermute x8, starting transfers between devices, passed_along(): return lax.ppermute(block, axis, route)  26.8 us
    dot_general x3, matrix products, attend_backward(): jnp.einsum('sp,skd->pkd', places, value_slots.reshape(slot_count, TILE, H...  24.7 us
    ppermute x8, waiting for transfers between devices, passed_along(): return lax.ppermute(block, axis, route)  24.1 us
  transfers between devices with their start and end apart: 18, of which 7 were waited for; matrix products, arithmetic and copies ran while one was open for 23% of the time, Pallas kernels for 0%

commit v1 on v0

--- a/solution.py
+++ b/solution.py
@@ -188,7 +188,9 @@
     key_grad = key_grad + returned[0]
     value_grad = value_grad + returned[1]
     summed = (
-        lax.psum(key_pool[:, span:].astype(jnp.bfloat16), "blk").astype(jnp.float32),
+        jnp.sum(lax.all_gather(key_pool[:, span:].astype(jnp.bfloat16), "blk"), axis=0).astype(
+            jnp.float32
+        ),
         lax.psum(value_pool[:, span:].astype(jnp.bfloat16), "blk").astype(jnp.float32),
     )
     owner_float = owner.astype(jnp.float32)

time: 904 us -> 939 us (1.039)
  blocking collectives: 0 us -> 14.4 us
  waiting for transfers between devices: 589 us -> 602 us
    all_gather x0 -> x1, waiting for transfers between devices: none -> 61.5 us  [per_device(): lax.all_gather(key_pool[:, span:].astype(jnp.bfloat16), 'blk')]
    psum x1, waiting for transfers between devices: 280 us -> 251 us  [per_device(): lax.psum(value_pool[:, span:].astype(jnp.bfloat16), 'blk')]
    ppermute x8, waiting for transfers between devices: 24.1 us -> 0.02 us  [passed_along(): return lax.ppermute(block, axis, route)]
    all_to_all x0 -> x1, blocking collectives: none -> 14.4 us  [per_device(): lax.all_to_all(merge_heads(attended), 'head', split_axis=0, concat_axis=1...]
  transfers between devices with their start and end apart: 18 -> 18, of which waited for: 7 -> 6; matrix products, arithmetic and copies ran while one was open for 23% -> 11% of each run, Pallas kernels for 0% -> 0%
where the time goes in v1:
time: 939 us; the launch traced here: 929 us
  waiting for transfers between devices  602 us (64%)
  local copies, waits for them, and re-layouts  95.7 us (10%)
  matrix products  95.6 us (10%)
  starting transfers between devices  66.7 us (7%)
  other arithmetic  29.1 us (3%)
  blocking collectives  14.4 us (2%)
  between operations  14.2 us (2%)
  loops' own time  11 us (1%)
    psum x1, waiting for transfers between devices, per_device(): lax.psum(global_keys.astype(jnp.bfloat16), 'blk').astype(jnp.float32)  263 us
    psum x1, waiting for transfers between devices, per_device(): lax.psum(value_pool[:, span:].astype(jnp.bfloat16), 'blk')  251 us
    all_gather x1, waiting for transfers between devices, per_device(): lax.all_gather(key_pool[:, span:].astype(jnp.bfloat16), 'blk')  61.5 us
    ppermute x8, starting transfers between devices, passed_along(): return lax.ppermute(block, axis, route)  29.2 us
    dot_general x3, matrix products, attend_backward(): jnp.einsum('sp,skd->pkd', places, value_slots.reshape(slot_count, TILE, H...  24.6 us
  transfers between devices with their start and end apart: 18, of which 6 were waited for; matrix products, arithmetic and copies ran while one was open for 11% of the time, Pallas kernels for 0%

profile of v1, /device:TPU:160, one launch (start us, length us, event | category | flops | bytes accessed | tf_op | source)
XLA Modules:
  0.0 929.1 jit_solution(6384496035808193703)
XLA Ops:
  9.5 5.9 all-to-all-start.1
  16.6 10.3 %all-to-all-done.1 = bf16[128,8,384]{0,2,1:T(8,128)(2,1)S(1)} async-done(((bf16[128,8,384]{0,2,1:T(8,128)(2,1)}), bf16[128,8,384]{0,2,1:T(8,128)(2,1)S(1)}, u32[]{:S(2)}, u32[]{:S(2)}) %all-to-all-start.1) | async-done | bytes 786464 | tf_op jit(solution)/shard_map/all_to_all | solution.py:108
  26.9 4.2 all-to-all-start.2
  32.2 10.5 %all-to-all-done.2 = bf16[128,8,384]{0,2,1:T(8,128)(2,1)S(1)} async-done(((bf16[128,8,384]{0,2,1:T(8,128)(2,1)}), bf16[128,8,384]{0,2,1:T(8,128)(2,1)S(1)}, u32[]{:S(2)}, u32[]{:S(2)}) %all-to-all-start.2) | async-done | bytes 786464 | tf_op jit(solution)/shard_map/all_to_all | solution.py:109
  42.7 4.2 all-to-all-start
  47.4 4.0 collective-permute-start.3
  61.8 7.8 collective-permute-start.1
  72.8 5.7 all-to-all-start.4
  80.1 262.5 %all-reduce.6.cloned.1.call-done = (bf16[3,2,128,128]{3,1,2,0:T(2,128)(2,1)}, bf16[3,2,128,128]{3,1,2,0:T(2,128)(2,1)}) async-done(((bf16[3,2,128,128]{3,1,2,0:T(2,128)(2,1)}, bf16[3,2,128,128]{3,1,2,0:T(2,128)(2,1)}), (bf16[3,2,128,128]{3,1,2,0:T(2,128)(2,1)}, bf16[3,2,128,128]{3,1,2,0:T(2,128)(2,1)})) %all-reduce.6.cloned.1.call-update) | async-done | bytes 393232 | tf_op jit(solution)/shard_map/psum | solution.py:142
  345.5 3.1 pad_maximum_fusion.3
  348.6 5.9 reshape_reshape.7
  354.5 3.1 pad_maximum_fusion.1
  359.8 3.3 pad_maximum_fusion.2
  363.1 5.9 reshape_reshape.6
  373.4 32.2 %while.26 = (s32[]{:T(128)}, bf16[3,8,128,128]{3,2,1,0:T(8,128)(2,1)}, f32[3,8,128,1,1]{2,1,4,3,0:T(8,128)S(1)}, bf16[3,8,128,128]{3,2,1,0:T(8,128)(2,1)}, bf16[...) while((s32[]{:T(128)}, ...), condition=%wide.region_6.8_spmd, body=%wide.region_3.7_spmd.sunk | while | flops 615907776 | bytes 41720132 | solution.py:159
  375.0 2.4 gather_fusion
  385.8 2.4 gather_fusion
  396.5 2.4 gather_fusion
  405.6 115.5 %while.27 = (s32[]{:T(128)}, bf16[3,8,128,128]{2,3,0,1:T(8,128)(2,1)}, f32[3,26,128,128]{3,1,2,0:T(8,128)}, f32[3,26,128,128]{3,1,2,0:T(8,128)}, bf16[3,8,128,12...) while((s32[]{:T(128)}, ...), condition=%wide.region_9.11_spmd, body=%wide.region_7.10_spmd.sunk | while | flops 2260996352 | bytes 105939144 | solution.py:160
  420.4 2.4 gather_fusion.2
  422.8 2.4 gather_fusion.3
  430.8 3.4 fusion.140
  435.2 8.2 bitcast_dynamic-update-slice_fusion.8
  445.3 6.0 bitcast_dynamic-update-slice_fusion.7
  455.3 2.4 gather_fusion.2
  457.7 2.4 gather_fusion.3
  465.7 3.4 fusion.140
  470.1 8.2 bitcast_dynamic-update-slice_fusion.8
  480.2 6.0 bitcast_dynamic-update-slice_fusion.7
  490.2 2.4 gather_fusion.2
  500.7 3.4 fusion.140
  505.0 8.2 bitcast_dynamic-update-slice_fusion.8
  515.1 6.0 bitcast_dynamic-update-slice_fusion.7
  521.1 3.5 convert.13
  527.2 3.5 convert.12
  533.9 14.4 %all_to_all.146 = bf16[8,128,384]{1,2,0:T(8,128)(2,1)} all-to-all(bf16[8,128,384]{1,2,0:T(8,128)(2,1)} %bitcast.244), channel_id=1, replica_groups=mesh['blk'=32,'head'=8] {'head'}, dimensions={0} | all-to-all | bytes 1572864 | tf_op jit(solution)/shard_map/all_to_all | solution.py:207
  548.3 5.7 all-to-all-start.5
  554.1 2.6 fusion.100
  556.7 5.7 collective-permute-start.6
  564.4 251.3 %all-reduce.4.cloned.1.call-done = bf16[3,2,128,128]{3,1,2,0:T(2,128)(2,1)} async-done(((bf16[3,2,128,128]{3,1,2,0:T(2,128)(2,1)}), bf16[3,2,128,128]{3,1,2,0:T(2,128)(2,1)}) %all-reduce.4.cloned.1.call-update) | async-done | bytes 196624 | tf_op jit(solution)/shard_map/psum | solution.py:194
  815.7 3.5 fusion.74
  819.2 2.4 copy.190
  821.6 5.7 all-to-all-start.7
  828.7 3.9 collective-permute-start.4
  834.6 61.5 %all-gather.3.cloned.1.call-done = bf16[96,2,128,128]{3,2,1,0:T(8,128)(2,1)} async-done(((bf16[3,2,128,128]{3,2,1,0:T(8,128)(2,1)}), bf16[96,2,128,128]{3,2,1,0:T(8,128)(2,1)}) %all-gather.3.cloned.1.call-update) | async-done | bytes 6291472 | tf_op jit(solution)/shard_map/all_gather | solution.py:191
  896.0 4.2 reduce_sum.40
  903.7 5.6 all-to-all-start.6
  915.1 6.1 all-to-all-done.6
  (187 shorter events, 115.5 us)
Async XLA Ops:
  7.2 8.3 copy-start.7
  9.5 21.5 %copy-start.8 = (bf16[128,3072]{1,0:T(8,128)(2,1)S(1)}, bf16[128,3072]{1,0:T(8,128)(2,1)}, u32[]{:S(2)}) copy-start(bf16[128,3072]{1,0:T(8,128)(2,1)} %param.11) | copy-start | bytes 2359300
  9.5 17.3 %all-to-all-start.1 = ((bf16[128,8,384]{0,2,1:T(8,128)(2,1)}), bf16[128,8,384]{0,2,1:T(8,128)(2,1)S(1)}, u32[]{:S(2)}, u32[]{:S(2)}) async-start(bf16[128,8,384]{0,2,1:T(8,128)(2,1)} %bitcast.39), calls=%async_computation.1 | async-start | bytes 1572864 | tf_op jit(solution)/shard_map/all_to_all | solution.py:108
  16.6 30.3 %copy-start.12 = (s32[3,256,9]{1,0,2:T(4,128)S(1)}, s32[3,256,9]{1,0,2:T(4,128)}, u32[]{:S(2)}) copy-start(s32[3,256,9]{1,0,2:T(4,128)} %param.15) | copy-start | bytes 82948
  26.9 15.8 %all-to-all-start.2 = ((bf16[128,8,384]{0,2,1:T(8,128)(2,1)}), bf16[128,8,384]{0,2,1:T(8,128)(2,1)S(1)}, u32[]{:S(2)}, u32[]{:S(2)}) async-start(bf16[128,8,384]{0,2,1:T(8,128)(2,1)} %bitcast.50), calls=%async_computation.2 | async-start | bytes 1572864 | tf_op jit(solution)/shard_map/all_to_all | solution.py:109
  42.7 30.2 %all-to-all-start = ((bf16[128,8,384]{0,2,1:T(8,128)(2,1)}), bf16[128,8,384]{0,2,1:T(8,128)(2,1)S(1)}, u32[]{:S(2)}, u32[]{:S(2)}) async-start(bf16[128,8,384]{0,2,1:T(8,128)(2,1)} %bitcast.35), calls=%async_computation | async-start | bytes 1572864 | tf_op jit(solution)/shard_map/all_to_all | solution.py:107
  46.9 295.7 %all-reduce.6.cloned.1.call-start = ((), (), s32[]{:S(2)}) async-start(), calls=%async_computation.10 | async-start | bytes 786432 | tf_op jit(solution)/shard_map/psum | solution.py:142
  47.0 13.6 %copy-start.10 = (s32[3,1,2]{2,0,1:T(4,128)}, s32[3,1,2]{2,0,1:T(4,128)S(1)}, u32[]{:S(2)}) copy-start(s32[3,1,2]{2,0,1:T(4,128)S(1)} %copy.204) | copy-start | bytes 76
  47.0 11.1 %copy-start.13 = (s32[8]{0:T(128)}, s32[8]{0:T(128)S(1)}, u32[]{:S(2)}) copy-start(s32[8]{0:T(128)S(1)} %iota_add_fusion) | copy-start | bytes 100
  47.4 298.2 %collective-permute-start.3 = (bf16[1024,384]{1,0:T(8,128)(2,1)S(1)}, bf16[1024,384]{1,0:T(8,128)(2,1)}, u32[]{:S(2)}, u32[]{:S(2)}) collective-permute-start(bf16[1024,384]{1,0:T(8,128)(2,1)S(1)} %bitcast.237), channel_id=1, source_target_pairs={{8,0},{16,8},{24,16},{32,24},{40,32},{48,40},{56,48},{64,56},{72,6... | collective-permute-start | bytes 2359304 | tf_op jit(solution)/shard_map/ppermute | solution.py:15
  51.3 294.2 %collective-permute-start.2 = (bf16[1024,384]{1,0:T(8,128)(2,1)S(1)}, bf16[1024,384]{1,0:T(8,128)(2,1)}, u32[]{:S(2)}, u32[]{:S(2)}) collective-permute-start(bf16[1024,384]{1,0:T(8,128)(2,1)S(1)} %bitcast.238), channel_id=1, source_target_pairs={{0,8},{8,16},{16,24},{24,32},{32,40},{40,48},{48,56},{56,64},{64,7... | collective-permute-start | bytes 2359304 | tf_op jit(solution)/shard_map/ppermute | solution.py:15
  58.1 13.6 %copy-start.9 = (bf16[128,3072]{1,0:T(8,128)(2,1)S(1)}, bf16[128,3072]{1,0:T(8,128)(2,1)}, u32[]{:S(2)}) copy-start(bf16[128,3072]{1,0:T(8,128)(2,1)} %param.14) | copy-start | bytes 2359300
  61.8 298.0 %collective-permute-start.1 = (bf16[1024,384]{1,0:T(8,128)(2,1)}, bf16[1024,384]{1,0:T(8,128)(2,1)}, u32[]{:S(2)}, u32[]{:S(2)}) collective-permute-start(bf16[1024,384]{1,0:T(8,128)(2,1)} %bitcast.41), channel_id=1, source_target_pairs={{8,0},{16,8},{24,16},{32,24},{40,32},{48,40},{56,48},{64,56},{72,6... | collective-permute-start | bytes 2359304 | tf_op jit(solution)/shard_map/ppermute | solution.py:15
  69.7 290.1 %collective-permute-start = (bf16[1024,384]{1,0:T(8,128)(2,1)}, bf16[1024,384]{1,0:T(8,128)(2,1)}, u32[]{:S(2)}, u32[]{:S(2)}) collective-permute-start(bf16[1024,384]{1,0:T(8,128)(2,1)} %bitcast.41), channel_id=1, source_target_pairs={{0,8},{8,16},{16,24},{24,32},{32,40},{40,48},{48,56},{56,64},{64,7... | collective-permute-start | bytes 2359304 | tf_op jit(solution)/shard_map/ppermute | solution.py:15
  72.8 332.8 %all-to-all-start.4 = ((bf16[128,8,384]{0,2,1:T(8,128)(2,1)}), bf16[128,8,384]{0,2,1:T(8,128)(2,1)}, u32[]{:S(2)}, u32[]{:S(2)}) async-start(bf16[128,8,384]{0,2,1:T(8,128)(2,1)} %bitcast.66), calls=%async_computation.4 | async-start | bytes 1572864 | tf_op jit(solution)/shard_map/all_to_all | solution.py:110
  78.5 737.2 %all-reduce.4.cloned.1.call-start = ((), (), s32[]{:S(2)}) async-start(), calls=%async_computation.8 | async-start | bytes 393216 | tf_op jit(solution)/shard_map/psum | solution.py:194
  380.3 1.7 copy-start.1
  391.0 1.7 copy-start.1
  401.8 1.7 copy-start.1
  422.8 2.4 copy-start
  425.2 2.0 copy-start.2
  429.4 1.4 copy-start.3
  435.2 8.2 copy-start.4
  457.7 2.4 copy-start
  460.1 2.0 copy-start.2
  464.3 1.4 copy-start.3
  470.1 8.2 copy-start.4
  492.6 2.4 copy-start
  495.0 2.1 copy-start.2
  499.2 1.4 copy-start.3
  505.0 8.2 copy-start.4
  524.6 1.7 copy-start.5
  527.1 368.9 %all-gather.3.cloned.1.call-start = ((), (), s32[]{:S(2)}) async-start(), calls=%async_computation.9 | async-start | bytes 6488064 | tf_op jit(solution)/shard_map/all_gather | solution.py:191
  548.3 267.4 %copy-start.11 = (s32[3,1,2]{2,0,1:T(4,128)S(1)}, s32[3,1,2]{2,0,1:T(4,128)}, u32[]{:S(2)}) copy-start(s32[3,1,2]{2,0,1:T(4,128)} %copy-done.10) | copy-start | bytes 76
  548.3 267.4 %copy-start.14 = (s32[8]{0:T(128)S(1)}, s32[8]{0:T(128)}, u32[]{:S(2)}) copy-start(s32[8]{0:T(128)} %copy-done.13) | copy-start | bytes 100
  548.3 273.3 %all-to-all-start.5 = ((bf16[8,128,384]{1,2,0:T(8,128)(2,1)}), bf16[8,128,384]{1,2,0:T(8,128)(2,1)}, u32[]{:S(2)}, u32[]{:S(2)}) async-start(bf16[8,128,384]{1,2,0:T(8,128)(2,1)} %bitcast.245), calls=%async_computation.5 | async-start | bytes 1572864 | tf_op jit(solution)/shard_map/all_to_all | solution.py:208
  556.7 259.0 %collective-permute-start.6 = (bf16[3,8,128,128]{3,1,2,0:T(8,128)(2,1)}, bf16[3,8,128,128]{3,1,2,0:T(8,128)(2,1)}, u32[]{:S(2)}, u32[]{:S(2)}) collective-permute-start(bf16[3,8,128,128]{3,1,2,0:T(8,128)(2,1)} %get-tuple-element.267), channel_id=1, source_target_pairs={{8,0},{16,8},{24,16},{32,24},{40,32},{48,40},{56,48},{64,56},{72,6... | collective-permute-start | bytes 2359304 | tf_op jit(solution)/shard_map/ppermute | solution.py:15
  562.4 253.3 %collective-permute-start.7 = (bf16[3,8,128,128]{3,1,2,0:T(8,128)(2,1)}, bf16[3,8,128,128]{3,1,2,0:T(8,128)(2,1)}, u32[]{:S(2)}, u32[]{:S(2)}) collective-permute-start(bf16[3,8,128,128]{3,1,2,0:T(8,128)(2,1)} %get-tuple-element.268), channel_id=1, source_target_pairs={{0,8},{8,16},{16,24},{24,32},{32,40},{40,48},{48,56},{56,64},{64,7... | collective-permute-start | bytes 2359304 | tf_op jit(solution)/shard_map/ppermute | solution.py:15
  821.6 82.1 %all-to-all-start.7 = ((bf16[8,128,384]{1,2,0:T(8,128)(2,1)}), bf16[8,128,384]{1,2,0:T(8,128)(2,1)}, u32[]{:S(2)}, u32[]{:S(2)}) async-start(bf16[8,128,384]{1,2,0:T(8,128)(2,1)} %bitcast.242), calls=%async_computation.7 | async-start | bytes 1572864 | tf_op jit(solution)/shard_map/all_to_all | solution.py:210
  828.7 71.5 %collective-permute-start.4 = (bf16[3,8,128,128]{3,1,2,0:T(8,128)(2,1)}, bf16[3,8,128,128]{3,1,2,0:T(8,128)(2,1)S(1)}, u32[]{:S(2)}, u32[]{:S(2)}) collective-permute-start(bf16[3,8,128,128]{3,1,2,0:T(8,128)(2,1)} %get-tuple-element.269), channel_id=1, source_target_pairs={{8,0},{16,8},{24,16},{32,24},{40,32},{48,40},{56,48},{64,56},{72,6... | collective-permute-start | bytes 2359304 | tf_op jit(solution)/shard_map/ppermute | solution.py:15
  832.6 67.6 %collective-permute-start.5 = (bf16[3,8,128,128]{3,1,2,0:T(8,128)(2,1)}, bf16[3,8,128,128]{3,1,2,0:T(8,128)(2,1)S(1)}, u32[]{:S(2)}, u32[]{:S(2)}) collective-permute-start(bf16[3,8,128,128]{3,1,2,0:T(8,128)(2,1)} %get-tuple-element.270), channel_id=1, source_target_pairs={{0,8},{8,16},{16,24},{24,32},{32,40},{40,48},{48,56},{56,64},{64,7... | collective-permute-start | bytes 2359304 | tf_op jit(solution)/shard_map/ppermute | solution.py:15
  902.3 7.0 copy-start.6
  903.7 17.5 %all-to-all-start.6 = ((bf16[8,128,384]{1,2,0:T(8,128)(2,1)}), bf16[8,128,384]{1,2,0:T(8,128)(2,1)S(1)}, u32[]{:S(2)}, u32[]{:S(2)}) async-start(bf16[8,128,384]{1,2,0:T(8,128)(2,1)} %bitcast.76), calls=%async_computation.6 | async-start | bytes 1572864 | tf_op jit(solution)/shard_map/all_to_all | solution.py:209
Sparse Core Ops, SparseCore 0:
  60.5 282.0 all-reduce.5
  527.3 288.3 all-reduce.3
  818.8 77.1 all-gather.2
